TPU v7x, 128 devices: a whole 4x4x4 slice. The times are simulated.
128 devices in a mesh: period: 4 (over x_hi, core), bus: 32 (over z, x_lo, y).
Axes of the slice: x: 4 (x_hi: 2, x_lo: 2; x = x_hi * 2 + x_lo), y: 4, z: 4, core: 2. Of those that a mesh axis runs over, the one named last changes fastest.
Arguments:
- gain: bfloat16 [4, 2048, 2048], P('period', 'bus'), may hold values from -0.15 to 1.15
- schur: bfloat16 [4, 2048, 2048], P('period', 'bus'), may hold values from -0.0625 to 0.0625
- inverse_blocks: bfloat16 [4, 10240, 320], P('period', 'bus'), may hold values from -0.3125 to 0.3125
- sensitivity: bfloat16 [10240, 2048], P('bus'), may hold values from -0.109375 to 0.109375
- residual_bus: float32 [4, 10240, 512], P('period', 'bus'), may hold values from -6 to 6
- unit_rhs: float32 [4, 2048, 512], P('period', 'bus'), may hold values from -6 to 6
- start_state: float32 [2048, 512], P('bus'), may hold values from -6 to 6
- active_set: int32 [4, 10240], P('period', 'bus'), may hold values 0 or 1
- unit_bus: int32 [2048], replicated, may hold values from 0 to 10239
Outputs:
- storage_path: float32 [4, 2048, 512], P('period', 'bus')
- costate: float32 [4, 2048, 512], P('period', 'bus')
- bus_update: float32 [4, 10240, 512], P('period', 'bus')
All inputs are finite; a program needn't handle non-finite values. No bound on the sum of `active_set` on one device may be relied on, other than what follows from the above.
Results may differ from a plain program's by a relative error of at most 0.008.
Values may be sent and summed in bfloat16 or wider, within the bound.
A program may use at most 64 MiB of HBM per device.

v0:
```python
import jax
import jax.numpy as jnp
from jax import lax
from jax.sharding import PartitionSpec as P


def passed_along(block, axis, distance):
    devices = range(lax.axis_size(axis))
    route = [(i - distance, i) for i in devices if i - distance in devices]
    return lax.ppermute(block, axis, route)


def body(
    gain,
    schur,
    inverse_blocks,
    sensitivity,
    residual_bus,
    unit_rhs,
    start_state,
    active_set,
    unit_bus,
):
    per_dev, unit_rows, total_units = gain.shape
    bus_rows = inverse_blocks.shape[1]
    rhs_cols = residual_bus.shape[2]
    groups = lax.axis_size("period")
    period_rank = lax.axis_index("period")
    bus_rank = lax.axis_index("bus")
    weighted = residual_bus * (1.0 + 3.0 * active_set[:, :, None].astype(jnp.float32))
    net_in = weighted.astype(jnp.bfloat16)
    bus_solve = jnp.einsum(
        "tij,tjr->tir", inverse_blocks, net_in, preferred_element_type=jnp.float32
    ).astype(jnp.bfloat16)
    solve_flat = jnp.transpose(bus_solve, (1, 0, 2)).reshape(bus_rows, per_dev * rhs_cols)
    reduced = lax.psum_scatter(
        lax.dot_general(
            sensitivity, solve_flat, (((0,), (0,)), ((), ())), preferred_element_type=jnp.float32
        ),
        "bus",
        scatter_dimension=0,
        tiled=True,
    )
    unit_right = unit_rhs + jnp.transpose(reduced.reshape(unit_rows, per_dev, rhs_cols), (1, 0, 2))
    blocks_count = 1
    block_cols = rhs_cols // blocks_count
    section_count = groups + blocks_count - 1
    costate = jnp.zeros((per_dev, unit_rows, rhs_cols), jnp.float32)
    outgoing = jnp.zeros((unit_rows, block_cols), jnp.float32)
    for section_index in range(section_count):
        incoming = passed_along(outgoing.astype(jnp.bfloat16), "period", -1).astype(outgoing.dtype)
        block_index = section_index - (groups - 1 - period_rank)
        is_valid = (block_index >= 0) & (block_index < blocks_count)
        later = incoming
        for local_step in reversed(range(per_dev)):
            rounded = later.astype(jnp.bfloat16)

            def transposed(row_start, row_count, weights=gain[local_step], vector=rounded):
                return lax.dot_general(
                    weights, vector, (((0,), (0,)), ((), ())), preferred_element_type=jnp.float32
                )

            summed = lax.psum_scatter(
                transposed(jnp.int32(0), unit_rows * lax.axis_size("bus")),
                "bus",
                scatter_dimension=0,
                tiled=True,
            )
            current = unit_right[local_step] + summed
            costate = jnp.where(is_valid, current[None], costate)
            later = current
        outgoing = later
    costate_round = costate.astype(jnp.bfloat16)
    bus_ids = bus_rank * bus_rows + jnp.arange(bus_rows, dtype=jnp.int32)
    placement = (unit_bus[None, :] == bus_ids[:, None]).astype(jnp.bfloat16)
    storage_path = jnp.zeros((per_dev, unit_rows, rhs_cols), jnp.float32)
    bus_update = jnp.zeros((per_dev, bus_rows, rhs_cols), jnp.float32)
    outgoing = jnp.zeros((unit_rows, block_cols), jnp.float32)
    for section_index in range(section_count):
        incoming = passed_along(outgoing.astype(jnp.bfloat16), "period", 1).astype(outgoing.dtype)
        block_index = section_index - period_rank
        is_valid = (block_index >= 0) & (block_index < blocks_count)
        current = jnp.where(period_rank == 0, start_state, incoming)
        local_step = 0
        rounded = current.astype(jnp.bfloat16)
        own_costate = costate_round[local_step]
        whole_state = lax.all_gather(rounded, "bus", axis=0, tiled=True)
        whole_costate = lax.all_gather(own_costate, "bus", axis=0, tiled=True)
        coupling = jnp.dot(schur[local_step], whole_costate, preferred_element_type=jnp.float32)
        injection = jnp.dot(placement, whole_state, preferred_element_type=jnp.float32)
        network = (weighted[local_step] - injection).astype(jnp.bfloat16)
        angle = jnp.dot(inverse_blocks[local_step], network, preferred_element_type=jnp.float32)
        advanced = (
            jnp.dot(gain[local_step], whole_state, preferred_element_type=jnp.float32) - coupling
        )
        storage_path = jnp.where(is_valid, advanced[None], storage_path)
        bus_update = jnp.where(is_valid, angle[None], bus_update)
        current = advanced
        outgoing = current
    return (storage_path, costate, bus_update)


def solution(mesh):
    placed = (
        P("period", "bus", None),
        P("period", "bus", None),
        P("period", "bus", None),
        P("bus", None),
        P("period", "bus", None),
        P("period", "bus", None),
        P("bus", None),
        P("period", "bus"),
        P(),
    )
    return jax.shard_map(
        body,
        mesh=mesh,
        in_specs=placed,
        out_specs=(P("period", "bus", None), P("period", "bus", None), P("period", "bus", None)),
        check_vma=False,
    )
```

profile of v0, /device:TPU:0, one launch (start us, length us, event | category | flops | bytes accessed | tf_op | source)
XLA Modules:
  0.0 1705.1 jit_solution(13985205716786645269)
XLA Ops:
  8.5 4.9 convolution_bitcast_fusion.4
  13.4 5.3 copy.22
  18.8 1.3 collective-permute-start.1
  20.1 1.8 collective-permute-done.1
  22.0 2.7 convolution_bitcast_fusion.3
  24.7 5.4 copy.24
  30.2 159.3 %reduce-scatter.16.cloned.1.call-done = f32[64,512]{1,0:T(8,128)} async-done(((f32[2048,512]{1,0:T(8,128)}), f32[64,512]{1,0:T(8,128)}) %reduce-scatter.16.cloned.1.call-update) | async-done | bytes 131088 | tf_op jit(solution)/shard_map/reduce_scatter | solution.py:36
  189.6 167.7 %reduce-scatter.18.cloned.1.call-done = f32[64,512]{1,0:T(8,128)} async-done(((f32[2048,512]{1,0:T(8,128)}), f32[64,512]{1,0:T(8,128)}) %reduce-scatter.18.cloned.1.call-update) | async-done | bytes 131088 | tf_op jit(solution)/shard_map/reduce_scatter | solution.py:63
  357.3 1.0 fusion.91
  358.3 1.3 collective-permute-start.2
  359.6 1.8 collective-permute-done.2
  361.4 2.8 convolution_bitcast_fusion.2
  364.2 5.3 copy.26
  369.6 166.2 %reduce-scatter.20.cloned.1.call-done = f32[64,512]{1,0:T(8,128)} async-done(((f32[2048,512]{1,0:T(8,128)}), f32[64,512]{1,0:T(8,128)}) %reduce-scatter.20.cloned.1.call-update) | async-done | bytes 131088 | tf_op jit(solution)/shard_map/reduce_scatter | solution.py:63
  535.8 0.9 fusion.92
  536.7 1.3 collective-permute-start.3
  538.0 1.8 collective-permute-done.3
  539.8 2.8 convolution_bitcast_fusion.1
  542.6 5.3 copy.28
  548.0 165.6 %reduce-scatter.22.cloned.1.call-done = f32[64,512]{1,0:T(8,128)} async-done(((f32[2048,512]{1,0:T(8,128)}), f32[64,512]{1,0:T(8,128)}) %reduce-scatter.22.cloned.1.call-update) | async-done | bytes 131088 | tf_op jit(solution)/shard_map/reduce_scatter | solution.py:63
  713.6 0.9 fusion.93
  714.5 1.3 collective-permute-start.4
  715.8 1.8 collective-permute-done.4
  717.6 2.8 convolution_bitcast_fusion
  720.4 5.3 copy.30
  725.9 166.4 %reduce-scatter.24.cloned.1.call-done = f32[64,512]{1,0:T(8,128)} async-done(((f32[2048,512]{1,0:T(8,128)}), f32[64,512]{1,0:T(8,128)}) %reduce-scatter.24.cloned.1.call-update) | async-done | bytes 131088 | tf_op jit(solution)/shard_map/reduce_scatter | solution.py:63
  892.3 1.6 fusion.94
  894.0 1.3 collective-permute-start
  896.9 146.7 %all-gather.8.cloned.1.call-done = bf16[2048,512]{1,0:T(8,128)(2,1)} async-done(((bf16[64,512]{1,0:T(8,128)(2,1)}), bf16[2048,512]{1,0:T(8,128)(2,1)}) %all-gather.8.cloned.1.call-update) | async-done | bytes 2097168 | tf_op jit(solution)/shard_map/all_gather | solution.py:88
  1043.7 2.1 fusion.74
  1045.7 153.3 %all-gather.6.cloned.1.call-done = bf16[2048,512]{1,0:T(8,128)(2,1)} async-done(((bf16[64,512]{1,0:T(8,128)(2,1)}), bf16[2048,512]{1,0:T(8,128)(2,1)}) %all-gather.6.cloned.1.call-update) | async-done | bytes 2097168 | tf_op jit(solution)/shard_map/all_gather | solution.py:87
  1199.1 2.1 convolution_subtract_fusion.3
  1201.2 1.3 collective-permute-start.5
  1202.5 0.9 collective-permute-done.5
  1204.1 158.0 %all-gather.10.cloned.1.call-done = bf16[2048,512]{1,0:T(8,128)(2,1)} async-done(((bf16[64,512]{1,0:T(8,128)(2,1)}), bf16[2048,512]{1,0:T(8,128)(2,1)}) %all-gather.10.cloned.1.call-update) | async-done | bytes 2097168 | tf_op jit(solution)/shard_map/all_gather | solution.py:87
  1362.1 2.1 convolution_subtract_fusion.2
  1364.2 1.4 collective-permute-start.6
  1365.7 0.9 collective-permute-done.6
  1367.3 158.0 %all-gather.12.cloned.1.call-done = bf16[2048,512]{1,0:T(8,128)(2,1)} async-done(((bf16[64,512]{1,0:T(8,128)(2,1)}), bf16[2048,512]{1,0:T(8,128)(2,1)}) %all-gather.12.cloned.1.call-update) | async-done | bytes 2097168 | tf_op jit(solution)/shard_map/all_gather | solution.py:87
  1525.3 2.1 convolution_subtract_fusion.1
  1527.4 1.3 collective-permute-start.7
  1528.7 0.9 collective-permute-done.7
  1530.3 3.7 fusion.51
  1534.0 3.6 fusion.48
  1537.6 150.7 %all-gather.14.cloned.1.call-done = bf16[2048,512]{1,0:T(8,128)(2,1)} async-done(((bf16[64,512]{1,0:T(8,128)(2,1)}), bf16[2048,512]{1,0:T(8,128)(2,1)}) %all-gather.14.cloned.1.call-update) | async-done | bytes 2097168 | tf_op jit(solution)/shard_map/all_gather | solution.py:87
  1688.4 3.6 fusion.45
  1692.0 2.7 fusion.54
  1694.7 3.6 fusion.31
  (53 shorter events, 5.4 us)
Async XLA Ops:
  7.2 1.3 copy-start
  7.2 182.4 %reduce-scatter.16.cloned.1.call-start = ((), (), s32[]{:S(2)}) async-start(), calls=%async_computation.10 | async-start | bytes 4325376 | tf_op jit(solution)/shard_map/reduce_scatter | solution.py:36
  18.7 3.2 copy-start.1
  18.8 338.5 %reduce-scatter.18.cloned.1.call-start = ((), (), s32[]{:S(2)}) async-start(), calls=%async_computation.11 | async-start | bytes 4325376 | tf_op jit(solution)/shard_map/reduce_scatter | solution.py:63
  18.8 3.1 collective-permute-start.1
  30.2 327.1 %copy-start.9 = (f32[1,64,512]{2,1,0:T(8,128)S(1)}, f32[1,64,512]{2,1,0:T(8,128)}, u32[]{:S(2)}) copy-start(f32[1,64,512]{2,1,0:T(8,128)} %param.14) | copy-start | bytes 393220
  30.2 505.6 %reduce-scatter.20.cloned.1.call-start = ((), (), s32[]{:S(2)}) async-start(), calls=%async_computation.12 | async-start | bytes 4325376 | tf_op jit(solution)/shard_map/reduce_scatter | solution.py:63
  358.3 3.1 collective-permute-start.2
  369.5 344.0 %reduce-scatter.22.cloned.1.call-start = ((), (), s32[]{:S(2)}) async-start(), calls=%async_computation.13 | async-start | bytes 4325376 | tf_op jit(solution)/shard_map/reduce_scatter | solution.py:63
  536.7 3.1 collective-permute-start.3
  547.9 344.4 %reduce-scatter.24.cloned.1.call-start = ((), (), s32[]{:S(2)}) async-start(), calls=%async_computation.14 | async-start | bytes 4325376 | tf_op jit(solution)/shard_map/reduce_scatter | solution.py:63
  714.5 3.1 collective-permute-start.4
  725.7 166.6 %copy-start.4 = (f32[64,512]{1,0:T(8,128)S(1)}, f32[64,512]{1,0:T(8,128)}, u32[]{:S(2)}) copy-start(f32[64,512]{1,0:T(8,128)} %reduce-scatter.20.cloned.1.call-done) | copy-start | bytes 393220
  725.7 166.6 %copy-start.5 = (f32[64,512]{1,0:T(8,128)S(1)}, f32[64,512]{1,0:T(8,128)}, u32[]{:S(2)}) copy-start(f32[64,512]{1,0:T(8,128)} %reduce-scatter.22.cloned.1.call-done) | copy-start | bytes 393220
  725.7 166.6 %copy-start.6 = (f32[64,512]{1,0:T(8,128)S(1)}, f32[64,512]{1,0:T(8,128)}, u32[]{:S(2)}) copy-start(f32[64,512]{1,0:T(8,128)} %reduce-scatter.18.cloned.1.call-done) | copy-start | bytes 393220
  725.7 170.5 %copy-start.2 = (f32[64,512]{1,0:T(8,128)S(1)}, f32[64,512]{1,0:T(8,128)}, u32[]{:S(2)}) copy-start(f32[64,512]{1,0:T(8,128)} %param.15) | copy-start | bytes 393220
  725.7 317.9 %copy-start.7 = (bf16[1,64,2048]{2,1,0:T(8,128)(2,1)S(1)}, bf16[1,64,2048]{2,1,0:T(8,128)(2,1)}, u32[]{:S(2)}) copy-start(bf16[1,64,2048]{2,1,0:T(8,128)(2,1)} %param.10) | copy-start | bytes 786436
  725.8 317.9 %all-gather.8.cloned.1.call-start = ((), (), s32[]{:S(2)}) async-start(), calls=%async_computation.6 | async-start | bytes 2162688 | tf_op jit(solution)/shard_map/all_gather | solution.py:88
  894.0 305.1 %all-gather.6.cloned.1.call-start = ((), (), s32[]{:S(2)}) async-start(), calls=%async_computation.5 | async-start | bytes 2162688 | tf_op jit(solution)/shard_map/all_gather | solution.py:87
  894.0 2.2 collective-permute-start
  896.9 465.2 %all-gather.10.cloned.1.call-start = ((), (), s32[]{:S(2)}) async-start(), calls=%async_computation.7 | async-start | bytes 2162688 | tf_op jit(solution)/shard_map/all_gather | solution.py:87
  1201.2 2.2 collective-permute-start.5
  1204.0 321.3 %all-gather.12.cloned.1.call-start = ((), (), s32[]{:S(2)}) async-start(), calls=%async_computation.8 | async-start | bytes 2162688 | tf_op jit(solution)/shard_map/all_gather | solution.py:87
  1364.2 166.1 %copy-start.3 = (f32[1,320,512]{2,1,0:T(8,128)S(1)}, f32[1,320,512]{2,1,0:T(8,128)}, u32[]{:S(2)}) copy-start(f32[1,320,512]{2,1,0:T(8,128)} %param.13) | copy-start | bytes 1966084
  1364.2 166.1 %copy-start.8 = (bf16[1,320,320]{2,1,0:T(8,128)(2,1)S(1)}, bf16[1,320,320]{2,1,0:T(8,128)(2,1)}, u32[]{:S(2)}) copy-start(bf16[1,320,320]{2,1,0:T(8,128)(2,1)} %param.11) | copy-start | bytes 614404
  1364.2 166.1 %copy-start.10 = (s32[2048]{0:T(1024)S(1)}, s32[2048]{0:T(1024)}, u32[]{:S(2)}) copy-start(s32[2048]{0:T(1024)} %param.17) | copy-start | bytes 24580
  1364.2 2.3 collective-permute-start.6
  1367.2 321.1 %all-gather.14.cloned.1.call-start = ((), (), s32[]{:S(2)}) async-start(), calls=%async_computation.9 | async-start | bytes 2162688 | tf_op jit(solution)/shard_map/all_gather | solution.py:87
  1527.4 2.2 collective-permute-start.7
Sparse Core Ops, SparseCore 0:
  18.9 170.6 reduce-scatter.15
  191.9 165.2 reduce-scatter.17
  369.7 166.0 reduce-scatter.19
  548.1 165.4 reduce-scatter.21
  725.9 166.3 reduce-scatter.23
  894.4 149.2 all-gather.7
  1045.9 153.1 all-gather.5
  1204.1 157.9 all-gather.9
  1367.3 157.9 all-gather.11
  1530.4 157.9 all-gather.13
where the time goes:
time: 1710 us
  waiting for transfers between devices  1600 us (94%)
  matrix products  41.4 us (2%)
  local copies, waits for them, and re-layouts  27.3 us (2%)
    reduce_scatter x4, waiting for transfers between devices, body(): lax.psum_scatter(transposed(jnp.int32(0), unit_rows * lax.axis_size('bus'...  666 us
    all_gather x4, waiting for transfers between devices, body(): whole_state = lax.all_gather(rounded, 'bus', axis=0, tiled=True)  620 us
    reduce_scatter x1, waiting for transfers between devices, body(): lax.psum_scatter(lax.dot_general(sensitivity, solve_flat, (((0,), (0,)),...  159 us
    all_gather x1, waiting for transfers between devices, body(): whole_costate = lax.all_gather(own_costate, 'bus', axis=0, tiled=True)  147 us
  transfers between devices with their start and end apart: 18, of which 18 were waited for; matrix products, arithmetic and copies ran while one was open for 1% of the time, Pallas kernels for 0%

commit v1 on v0

--- a/solution.py
+++ b/solution.py
@@ -2,6 +2,13 @@
 import jax.numpy as jnp
 from jax import lax
 from jax.sharding import PartitionSpec as P
+
+
+def all_by_exchange(shard, axis, d):
+    size = lax.axis_size(axis)
+    blocks = jnp.stack([shard for _ in range(size)])
+    blocks = lax.all_to_all(blocks, axis, split_axis=0, concat_axis=0)
+    return jnp.concatenate(blocks, axis=d)
 
 
 def passed_along(block, axis, distance):
@@ -84,7 +91,7 @@
         local_step = 0
         rounded = current.astype(jnp.bfloat16)
         own_costate = costate_round[local_step]
-        whole_state = lax.all_gather(rounded, "bus", axis=0, tiled=True)
+        whole_state = all_by_exchange(rounded, "bus", 0)
         whole_costate = lax.all_gather(own_costate, "bus", axis=0, tiled=True)
         coupling = jnp.dot(schur[local_step], whole_costate, preferred_element_type=jnp.float32)
         injection = jnp.dot(placement, whole_state, preferred_element_type=jnp.float32)

time: 1710 us -> 1190 us (0.70)
  waiting for transfers between devices: 1600 us -> 1010 us
  blocking collectives: 0 us -> 68.3 us
    all_gather x4 -> x0, waiting for transfers between devices: 620 us -> none  [body(): whole_state = lax.all_gather(rounded, 'bus', axis=0, tiled=True)]
    all_to_all x0 -> x2, blocking collectives: none -> 68.3 us  [all_by_exchange(): blocks = lax.all_to_all(blocks, axis, split_axis=0, concat_axis=0)]
    all_to_all x0 -> x2, waiting for transfers between devices: none -> 23 us  [all_by_exchange(): blocks = lax.all_to_all(blocks, axis, split_axis=0, concat_axis=0)]
  transfers between devices with their start and end apart: 18 -> 16, of which waited for: 18 -> 15; matrix products, arithmetic and copies ran while one was open for 1% -> 2% of each run, Pallas kernels for 0% -> 0%
where the time goes in v1:
time: 1190 us
  waiting for transfers between devices  1010 us (85%)
  blocking collectives  68.3 us (6%)
  matrix products  38.3 us (3%)
  local copies, waits for them, and re-layouts  33.7 us (3%)
  starting transfers between devices  24.4 us (2%)
  between operations  14.4 us (1%)
    reduce_scatter x4, waiting for transfers between devices, body(): lax.psum_scatter(transposed(jnp.int32(0), unit_rows * lax.axis_size('bus'...  665 us
    reduce_scatter x1, waiting for transfers between devices, body(): lax.psum_scatter(lax.dot_general(sensitivity, solve_flat, (((0,), (0,)),...  160 us
    all_gather x1, waiting for transfers between devices, body(): whole_costate = lax.all_gather(own_costate, 'bus', axis=0, tiled=True)  147 us
    all_to_all x2, blocking collectives, all_by_exchange(): blocks = lax.all_to_all(blocks, axis, split_axis=0, concat_axis=0)  68.3 us
    unnamed x33, local copies, waits for them, and re-layouts  30.1 us
  transfers between devices with their start and end apart: 16, of which 15 were waited for; matrix products, arithmetic and copies ran while one was open for 2% of the time, Pallas kernels for 0%

profile of v1, /device:TPU:0, one launch (start us, length us, event | category | flops | bytes accessed | tf_op | source)
XLA Modules:
  0.0 1190.5 jit_solution(438241025909549476)
XLA Ops:
  8.5 4.9 convolution_bitcast_fusion.4
  13.4 5.3 copy.22
  18.8 1.3 collective-permute-start.1
  20.1 1.8 collective-permute-done.1
  22.0 2.7 convolution_bitcast_fusion.3
  24.7 5.5 copy.24
  30.2 159.8 %reduce-scatter.16.cloned.1.call-done = f32[64,512]{1,0:T(8,128)} async-done(((f32[2048,512]{1,0:T(8,128)}), f32[64,512]{1,0:T(8,128)}) %reduce-scatter.16.cloned.1.call-update) | async-done | bytes 131088 | tf_op jit(solution)/shard_map/reduce_scatter | solution.py:43
  190.0 166.6 %reduce-scatter.18.cloned.1.call-done = f32[64,512]{1,0:T(8,128)} async-done(((f32[2048,512]{1,0:T(8,128)}), f32[64,512]{1,0:T(8,128)}) %reduce-scatter.18.cloned.1.call-update) | async-done | bytes 131088 | tf_op jit(solution)/shard_map/reduce_scatter | solution.py:70
  356.6 1.0 fusion.91
  357.6 1.3 collective-permute-start.2
  358.9 1.8 collective-permute-done.2
  360.7 2.8 convolution_bitcast_fusion.2
  363.5 5.3 copy.26
  368.9 166.1 %reduce-scatter.20.cloned.1.call-done = f32[64,512]{1,0:T(8,128)} async-done(((f32[2048,512]{1,0:T(8,128)}), f32[64,512]{1,0:T(8,128)}) %reduce-scatter.20.cloned.1.call-update) | async-done | bytes 131088 | tf_op jit(solution)/shard_map/reduce_scatter | solution.py:70
  535.0 0.9 fusion.92
  535.9 1.3 collective-permute-start.3
  537.2 1.8 collective-permute-done.3
  539.1 2.8 convolution_bitcast_fusion.1
  541.8 5.3 copy.28
  547.2 165.9 %reduce-scatter.22.cloned.1.call-done = f32[64,512]{1,0:T(8,128)} async-done(((f32[2048,512]{1,0:T(8,128)}), f32[64,512]{1,0:T(8,128)}) %reduce-scatter.22.cloned.1.call-update) | async-done | bytes 131088 | tf_op jit(solution)/shard_map/reduce_scatter | solution.py:70
  713.1 0.9 fusion.93
  714.0 1.3 collective-permute-start.4
  715.3 1.8 collective-permute-done.4
  717.2 2.8 convolution_bitcast_fusion
  720.0 5.3 copy.30
  725.4 166.3 %reduce-scatter.24.cloned.1.call-done = f32[64,512]{1,0:T(8,128)} async-done(((f32[2048,512]{1,0:T(8,128)}), f32[64,512]{1,0:T(8,128)}) %reduce-scatter.24.cloned.1.call-update) | async-done | bytes 131088 | tf_op jit(solution)/shard_map/reduce_scatter | solution.py:70
  891.7 1.6 fusion.94
  893.4 1.3 collective-permute-start
  895.6 1.6 stack.8
  897.2 4.9 all-to-all-start
  902.1 147.3 %all-gather.2.cloned.1.call-done = bf16[2048,512]{1,0:T(8,128)(2,1)} async-done(((bf16[64,512]{1,0:T(8,128)(2,1)}), bf16[2048,512]{1,0:T(8,128)(2,1)}) %all-gather.2.cloned.1.call-update) | async-done | bytes 2097168 | tf_op jit(solution)/shard_map/all_gather | solution.py:95
  1049.4 2.1 fusion.74
  1051.4 2.1 convolution_subtract_fusion.3
  1053.5 1.3 collective-permute-start.5
  1056.0 34.7 %all_to_all.20 = bf16[32,64,512]{2,1,0:T(8,128)(2,1)S(1)} all-to-all(bf16[32,64,512]{2,1,0:T(8,128)(2,1)S(1)} %stack.9), channel_id=1, replica_groups=mesh['period'=4,'bus'=32] {'bus'}, dimensions={0} | all-to-all | bytes 4194304 | tf_op jit(solution)/shard_map/all_to_all | solution.py:10
  1090.7 1.4 copy-done.3
  1092.6 2.7 collective-permute-start.6
  1096.5 33.6 %all_to_all.21 = bf16[32,64,512]{2,1,0:T(8,128)(2,1)S(1)} all-to-all(bf16[32,64,512]{2,1,0:T(8,128)(2,1)S(1)} %stack.10), channel_id=1, replica_groups=mesh['period'=4,'bus'=32] {'bus'}, dimensions={0} | all-to-all | bytes 4194304 | tf_op jit(solution)/shard_map/all_to_all | solution.py:10
  1130.1 1.4 copy-done.4
  1132.0 2.6 collective-permute-start.7
  1135.5 1.6 stack.11
  1137.1 6.2 all-to-all-start.3
  1143.3 3.6 fusion.51
  1146.9 3.7 fusion.48
  1150.6 23.0 %all-to-all-done.3 = bf16[32,64,512]{2,1,0:T(8,128)(2,1)} async-done(((bf16[32,64,512]{2,1,0:T(8,128)(2,1)}), bf16[32,64,512]{2,1,0:T(8,128)(2,1)}, u32[]{:S(2)}, u32[]{:S(2)}) %all-to-all-start.3) | async-done | bytes 2097184 | tf_op jit(solution)/shard_map/all_to_all | solution.py:10
  1173.6 3.6 fusion.45
  1177.2 2.8 fusion.54
  1180.1 3.6 fusion.31
  (57 shorter events, 6.7 us)
Async XLA Ops:
  7.2 1.3 copy-start
  7.2 182.8 %reduce-scatter.16.cloned.1.call-start = ((), (), s32[]{:S(2)}) async-start(), calls=%async_computation.10 | async-start | bytes 4325376 | tf_op jit(solution)/shard_map/reduce_scatter | solution.py:43
  18.7 3.2 copy-start.2
  18.8 337.8 %reduce-scatter.18.cloned.1.call-start = ((), (), s32[]{:S(2)}) async-start(), calls=%async_computation.11 | async-start | bytes 4325376 | tf_op jit(solution)/shard_map/reduce_scatter | solution.py:70
  18.8 3.1 collective-permute-start.1
  30.2 326.4 %copy-start.12 = (f32[1,64,512]{2,1,0:T(8,128)S(1)}, f32[1,64,512]{2,1,0:T(8,128)}, u32[]{:S(2)}) copy-start(f32[1,64,512]{2,1,0:T(8,128)} %param.14) | copy-start | bytes 393220
  30.2 504.8 %reduce-scatter.20.cloned.1.call-start = ((), (), s32[]{:S(2)}) async-start(), calls=%async_computation.12 | async-start | bytes 4325376 | tf_op jit(solution)/shard_map/reduce_scatter | solution.py:70
  357.6 3.1 collective-permute-start.2
  368.9 344.3 %reduce-scatter.22.cloned.1.call-start = ((), (), s32[]{:S(2)}) async-start(), calls=%async_computation.13 | async-start | bytes 4325376 | tf_op jit(solution)/shard_map/reduce_scatter | solution.py:70
  535.9 3.1 collective-permute-start.3
  547.2 344.5 %reduce-scatter.24.cloned.1.call-start = ((), (), s32[]{:S(2)}) async-start(), calls=%async_computation.14 | async-start | bytes 4325376 | tf_op jit(solution)/shard_map/reduce_scatter | solution.py:70
  714.0 3.1 collective-permute-start.4
  725.3 166.4 %copy-start.7 = (f32[64,512]{1,0:T(8,128)S(1)}, f32[64,512]{1,0:T(8,128)}, u32[]{:S(2)}) copy-start(f32[64,512]{1,0:T(8,128)} %reduce-scatter.20.cloned.1.call-done) | copy-start | bytes 393220
  725.3 166.4 %copy-start.8 = (f32[64,512]{1,0:T(8,128)S(1)}, f32[64,512]{1,0:T(8,128)}, u32[]{:S(2)}) copy-start(f32[64,512]{1,0:T(8,128)} %reduce-scatter.22.cloned.1.call-done) | copy-start | bytes 393220
  725.3 166.4 %copy-start.9 = (f32[64,512]{1,0:T(8,128)S(1)}, f32[64,512]{1,0:T(8,128)}, u32[]{:S(2)}) copy-start(f32[64,512]{1,0:T(8,128)} %reduce-scatter.18.cloned.1.call-done) | copy-start | bytes 393220
  725.3 170.3 %copy-start.5 = (f32[64,512]{1,0:T(8,128)S(1)}, f32[64,512]{1,0:T(8,128)}, u32[]{:S(2)}) copy-start(f32[64,512]{1,0:T(8,128)} %param.15) | copy-start | bytes 393220
  725.3 324.0 %all-gather.2.cloned.1.call-start = ((), (), s32[]{:S(2)}) async-start(), calls=%async_computation.9 | async-start | bytes 2162688 | tf_op jit(solution)/shard_map/all_gather | solution.py:95
  893.4 2.2 collective-permute-start
  897.2 152.2 %copy-start.10 = (bf16[1,64,2048]{2,1,0:T(8,128)(2,1)S(1)}, bf16[1,64,2048]{2,1,0:T(8,128)(2,1)}, u32[]{:S(2)}) copy-start(bf16[1,64,2048]{2,1,0:T(8,128)(2,1)} %param.10) | copy-start | bytes 786436
  897.2 154.3 %all-to-all-start = ((bf16[32,64,512]{2,1,0:T(8,128)(2,1)}), bf16[32,64,512]{2,1,0:T(8,128)(2,1)}, u32[]{:S(2)}, u32[]{:S(2)}) async-start(bf16[32,64,512]{2,1,0:T(8,128)(2,1)} %stack.8), calls=%async_computation | async-start | bytes 4194304 | tf_op jit(solution)/shard_map/all_to_all | solution.py:10
  1053.5 2.2 collective-permute-start.5
  1090.7 1.4 copy-start.3
  1092.6 3.6 collective-permute-start.6
  1130.1 1.4 copy-start.4
  1132.0 3.5 collective-permute-start.7
  1137.1 6.2 copy-start.6
  1137.1 6.2 copy-start.11
  1137.1 6.2 copy-start.13
  1137.1 36.5 %all-to-all-start.3 = ((bf16[32,64,512]{2,1,0:T(8,128)(2,1)}), bf16[32,64,512]{2,1,0:T(8,128)(2,1)}, u32[]{:S(2)}, u32[]{:S(2)}) async-start(bf16[32,64,512]{2,1,0:T(8,128)(2,1)} %stack.11), calls=%async_computation.3 | async-start | bytes 4194304 | tf_op jit(solution)/shard_map/all_to_all | solution.py:10
  1177.2 6.4 copy-start.1
Sparse Core Ops, SparseCore 0:
  18.9 171.0 reduce-scatter.15
  192.4 164.1 reduce-scatter.17
  369.0 165.9 reduce-scatter.19
  547.3 165.7 reduce-scatter.21
  725.4 166.2 reduce-scatter.23
  893.8 155.5 all-gather.1
